TPU v7x, 256 devices: a whole 4x4x8 slice. The times are simulated.
256 devices in a mesh: row: 64 (over y, z, x_hi), col: 4 (over x_lo, core).
Axes of the slice: x: 4 (x_hi: 2, x_lo: 2; x = x_hi * 2 + x_lo), y: 4, z: 8, core: 2. Of those that a mesh axis runs over, the one named last changes fastest.
Arguments:
- matrix_slab: float32 [16384, 2048], P('row', 'col'), may hold values from -6 to 6
- sketch_matrix: float32 [144, 16384], P(None, 'row'), may hold values from -0.046875 to 0.046875
- pivots: int32 [1, 128], replicated, may hold values from 128 to 1919, as said below
Outputs:
- sketches: float32 [1, 144, 2048], P(None, None, 'col')
- q_panels: float32 [1, 16384, 128], P(None, 'row')
- r_factors: float32 [1, 128, 2048], P(None, None, 'col')
- first_factors: float32 [1, 128, 128], replicated
- slab_out: float32 [16384, 2048], P('row', 'col')
Inputs may be any that keep to these rules, and one draw needn't show every extreme that they name: `pivots`: each row holds 128 different numbers.
All inputs are finite; a program needn't handle non-finite values.
Results may differ from a plain program's by a relative error of at most 0.0003.
Values sent between devices are 32-bit elements; how exact they have to be, the bound alone decides.
A program may use at most 64 MiB of HBM per device.

v0:
```python
import math
import jax
import jax.numpy as jnp
from jax import lax
from jax.sharding import PartitionSpec as P

PANEL = 128


def product(left, right):
    return jnp.dot(left, right, precision=lax.Precision.HIGHEST, preferred_element_type=jnp.float32)


def solve_right(lower, rhs):
    return lax.linalg.triangular_solve(lower, rhs, left_side=False, lower=True, transpose_a=True)


def pick_columns(array, local_ids, inside):
    width = array.shape[1]
    picked = jnp.take(array, jnp.clip(local_ids, 0, width - 1), axis=1)
    return jnp.where(inside[None, :], picked, jnp.float32(0.0))


def place_columns(array, local_ids, inside, values):
    target = jnp.where(inside, local_ids, array.shape[1])
    return array.at[:, target].set(values, mode="drop")


def shards(matrix_slab, sketch_matrix, pivots):
    rows_dev, col_width = matrix_slab.shape
    m_total = rows_dev * lax.axis_size("row")
    row_scale = math.sqrt(m_total)
    col_first = lax.axis_index("col") * col_width
    column = col_first + jnp.arange(col_width, dtype=jnp.int32)
    current = matrix_slab
    sketch = lax.psum(product(sketch_matrix, current), "row")
    sketch_list = [sketch]
    pivot_ids = 0 + pivots[0]
    slot_ids = 0 + jnp.arange(PANEL, dtype=jnp.int32)
    pivot_local = pivot_ids - col_first
    slot_local = slot_ids - col_first
    pivot_inside = (pivot_local >= 0) & (pivot_local < col_width)
    slot_inside = (slot_local >= 0) & (slot_local < col_width)
    in_slots = (column >= 0) & (column < PANEL)
    panel_cols, lead_cols = lax.psum(
        (
            pick_columns(current, pivot_local, pivot_inside),
            pick_columns(current, slot_local, slot_inside),
        ),
        "col",
    )
    swapped = place_columns(
        place_columns(current, slot_local, slot_inside, panel_cols),
        pivot_local,
        pivot_inside,
        lead_cols,
    )
    gram_one = lax.psum(product(panel_cols.T, panel_cols), "row")
    factor_one = jnp.linalg.cholesky(gram_one)
    basis_one = solve_right(factor_one, panel_cols)
    gram_two = lax.psum(product(basis_one.T, basis_one), "row")
    factor_two = jnp.linalg.cholesky(gram_two)
    basis = solve_right(factor_two, basis_one)
    r_factor = product(factor_two.T, factor_one.T)
    projected = lax.psum(product(basis.T, swapped), "row")
    r_block = place_columns(projected, slot_local, slot_inside, r_factor)
    current = jnp.where(in_slots[None, :], jnp.float32(0.0), swapped - product(basis, projected))
    q_list = [basis * row_scale]
    r_list = [r_block / row_scale]
    first_list = [factor_one.T / row_scale]
    return (
        jnp.stack(sketch_list),
        jnp.stack(q_list),
        jnp.stack(r_list),
        jnp.stack(first_list),
        current,
    )


def solution(mesh):
    in_specs = (P("row", "col"), P(None, "row"), P())
    out_specs = (
        P(None, None, "col"),
        P(None, "row", None),
        P(None, None, "col"),
        P(),
        P("row", "col"),
    )
    return jax.shard_map(shards, mesh=mesh, in_specs=in_specs, out_specs=out_specs, check_vma=False)
```

profile of v0, /device:TPU:32, one launch (start us, length us, event | category | flops | bytes accessed | tf_op | source)
XLA Modules:
  0.0 1997.1 jit_solution(17937217708790303102)
XLA Ops:
  7.2 0.0 copy-start
  7.2 0.0 all-reduce.13.cloned.1.call-start
  7.2 0.0 copy-start.8
  7.2 0.7 copy-done.8
  8.0 1.2 copy.8
  9.2 0.8 gather_fusion
  10.0 0.8 gather_fusion.1
  10.8 0.8 bitcast_select_fusion.1
  11.5 0.8 bitcast_select_fusion
  12.3 0.0 all-reduce.13.cloned.1.call-update
  12.3 0.0 all-reduce.7.cloned.1.call-start
  12.4 44.1 %all-reduce.13.cloned.1.call-done = (f32[256,128]{0,1:T(8,128)}, f32[256,128]{0,1:T(8,128)}) async-done(((f32[256,128]{0,1:T(8,128)}, f32[256,128]{0,1:T(8,128)}), (f32[256,128]{0,1:T(8,128)}, f32[256,128]{0,1:T(8,128)})) %all-reduce.13.cloned.1.call-update) | async-done | bytes 262160 | tf_op jit(solution)/shard_map/psum | solution.py:45
  56.5 1.9 fusion.29
  58.4 0.0 all-reduce.7.cloned.1.call-update
  58.4 0.0 all-reduce.9.cloned.1.call-start
  58.5 619.8 %all-reduce.7.cloned.1.call-done = f32[128,128]{0,1:T(8,128)} async-done(((f32[128,128]{0,1:T(8,128)}), f32[128,128]{0,1:T(8,128)}) %all-reduce.7.cloned.1.call-update) | async-done | bytes 65552 | tf_op jit(solution)/shard_map/psum | solution.py:58
  678.2 0.0 copy-start.6
  678.2 1.0 copy.10
  679.2 0.0 copy-done.6
  679.3 11.7 cholesky.44
  691.0 0.0 copy-start.1
  691.0 0.0 copy-start.2
  691.0 0.6 compare_reduce_fusion.1
  691.7 0.7 multiply_bitcast_fusion.2
  692.3 9.8 custom-call.6
  702.2 0.0 copy-done.1
  702.2 0.3 convolution_bitcast_fusion.2
  702.5 0.9 fusion.30
  703.4 0.0 all-reduce.9.cloned.1.call-update
  703.4 0.0 all-reduce.11.cloned.1.call-start
  703.5 0.0 copy-done
  703.5 0.0 copy-done.2
  703.5 1.2 convolution_bitcast_fusion
  704.6 0.0 copy-start.7
  704.6 1.2 scatter_custom_fusion
  705.9 0.0 copy-done.7
  705.9 1.4 scatter_custom_fusion.1
  707.3 610.2 %all-reduce.9.cloned.1.call-done = f32[128,128]{0,1:T(8,128)} async-done(((f32[128,128]{0,1:T(8,128)}), f32[128,128]{0,1:T(8,128)}) %all-reduce.9.cloned.1.call-update) | async-done | bytes 65552 | tf_op jit(solution)/shard_map/psum | solution.py:61
  1317.6 0.0 copy-start.5
  1317.6 1.0 copy.12
  1318.6 0.0 copy-done.5
  1318.6 11.7 cholesky.55
  1330.4 0.7 compare_reduce_fusion
  1331.1 0.6 select_bitcast_fusion
  1331.7 9.8 custom-call.7
  1341.5 0.3 convolution_bitcast_fusion.1
  1341.8 1.3 fusion.31
  1343.2 0.0 all-reduce.11.cloned.1.call-update
  1343.2 0.2 copy.16
  1343.4 0.7 copy.19
  1344.2 0.8 copy.17
  1344.9 1.5 fusion.15
  1346.4 639.0 %all-reduce.11.cloned.1.call-done = (f32[1,144,512]{2,1,0:T(8,128)}, f32[128,512]{1,0:T(8,128)}) async-done(((f32[1,144,512]{2,1,0:T(8,128)}, f32[128,512]{1,0:T(8,128)}), (f32[1,144,512]{2,1,0:T(8,128)}, f32[128,512]{1,0:T(8,128)})) %all-reduce.11.cloned.1.call-update) | async-done | bytes 557072 | tf_op jit(solution)/shard_map/psum | solution.py:36
  1985.4 1.1 copy.15
  1986.5 1.0 scatter_fusion
  1987.5 0.0 copy-start.3
  1987.5 0.8 copy.18
  1988.4 0.1 copy-done.3
  1988.5 0.0 copy-start.4
  1988.5 1.4 fusion
  1989.9 0.0 copy-done.4
  1989.9 0.7 copy.31
  (14 shorter events, 0.2 us)
Async XLA Ops:
  7.2 696.3 %copy-start = (f32[144,256]{1,0:T(8,128)S(1)}, f32[144,256]{1,0:T(8,128)}, u32[]{:S(2)}) copy-start(f32[144,256]{1,0:T(8,128)} %param.9) | copy-start | bytes 442372
  7.2 49.3 %all-reduce.13.cloned.1.call-start = ((), (), s32[]{:S(2)}) async-start(), calls=%async_computation.3 | async-start | bytes 524288 | tf_op jit(solution)/shard_map/psum | solution.py:45
  7.2 0.7 copy-start.8
  12.3 665.9 %all-reduce.7.cloned.1.call-start = ((), (), s32[]{:S(2)}) async-start(), calls=%async_computation | async-start | bytes 131072 | tf_op jit(solution)/shard_map/psum | solution.py:58
  58.4 1259.2 %all-reduce.9.cloned.1.call-start = ((), (), s32[]{:S(2)}) async-start(), calls=%async_computation.1 | async-start | bytes 131072 | tf_op jit(solution)/shard_map/psum | solution.py:61
  678.2 1.0 copy-start.6
  691.0 11.2 copy-start.1
  691.0 12.5 copy-start.2
  703.4 1282.0 %all-reduce.11.cloned.1.call-start = ((), (), s32[]{:S(2)}) async-start(), calls=%async_computation.2 | async-start | bytes 1114112 | tf_op jit(solution)/shard_map/psum | solution.py:36
  704.6 1.2 copy-start.7
  1317.6 1.0 copy-start.5
  1987.5 1.0 copy-start.3
  1988.5 1.4 copy-start.4
Sparse Core Ops, SparseCore 0:
  12.4 44.0 all-reduce.12
  59.9 618.3 all-reduce.6
  703.5 613.9 all-reduce.8
  1343.3 642.0 all-reduce.10
where the time goes:
time: 2000 us
  waiting for transfers between devices  1910 us (96%)
  other arithmetic  47.4 us (2%)
    psum x1, waiting for transfers between devices, shards(): sketch = lax.psum(product(sketch_matrix, current), 'row')  639 us
    psum x1, waiting for transfers between devices, shards(): gram_one = lax.psum(product(panel_cols.T, panel_cols), 'row')  620 us
    psum x1, waiting for transfers between devices, shards(): gram_two = lax.psum(product(basis_one.T, basis_one), 'row')  610 us
    psum x1, waiting for transfers between devices, shards(): lax.psum((pick_columns(current, pivot_local, pivot_inside), pick_columns(...  44.1 us
  transfers between devices with their start and end apart: 4, of which 4 were waited for; matrix products, arithmetic and copies ran while one was open for 0% of the time, Pallas kernels for 0%

commit v1 on v0

--- a/solution.py
+++ b/solution.py
@@ -5,6 +5,12 @@
 from jax.sharding import PartitionSpec as P
 
 PANEL = 128
+
+
+def summed_here(x, axis):
+    terms = lax.all_gather(x, axis, axis=0, tiled=False)
+    summed = terms.sum(axis=0)
+    return summed
 
 
 def product(left, right):
@@ -58,7 +64,7 @@
     gram_one = lax.psum(product(panel_cols.T, panel_cols), "row")
     factor_one = jnp.linalg.cholesky(gram_one)
     basis_one = solve_right(factor_one, panel_cols)
-    gram_two = lax.psum(product(basis_one.T, basis_one), "row")
+    gram_two = summed_here(product(basis_one.T, basis_one), "row")
     factor_two = jnp.linalg.cholesky(gram_two)
     basis = solve_right(factor_two, basis_one)
     r_factor = product(factor_two.T, factor_one.T)

time: 2000 us -> 1510 us (0.76)
  waiting for transfers between devices: 1910 us -> 1420 us
    psum x1 -> x0, waiting for transfers between devices: 610 us -> none  [shards(): gram_two = lax.psum(product(basis_one.T, basis_one), 'row')]
    all_gather x0 -> x1, waiting for transfers between devices: none -> 120 us  [summed_here(): terms = lax.all_gather(x, axis, axis=0, tiled=False)]
  transfers between devices with their start and end apart: 4 -> 4, of which waited for: 4 -> 4; matrix products, arithmetic and copies ran while one was open for 0% -> 1% of each run, Pallas kernels for 0% -> 0%
where the time goes in v1:
time: 1510 us
  waiting for transfers between devices  1420 us (94%)
  other arithmetic  52 us (3%)
    psum x1, waiting for transfers between devices, shards(): sketch = lax.psum(product(sketch_matrix, current), 'row')  639 us
    psum x1, waiting for transfers between devices, shards(): gram_one = lax.psum(product(panel_cols.T, panel_cols), 'row')  620 us
    all_gather x1, waiting for transfers between devices, summed_here(): terms = lax.all_gather(x, axis, axis=0, tiled=False)  120 us
    psum x1, waiting for transfers between devices, shards(): lax.psum((pick_columns(current, pivot_local, pivot_inside), pick_columns(...  44.1 us
  transfers between devices with their start and end apart: 4, of which 4 were waited for; matrix products, arithmetic and copies ran while one was open for 1% of the time, Pallas kernels for 0%

profile of v1, /device:TPU:32, one launch (start us, length us, event | category | flops | bytes accessed | tf_op | source)
XLA Modules:
  0.0 1512.2 jit_solution(7402550568766089230)
XLA Ops:
  7.2 0.0 copy-start
  7.2 0.0 copy-start.3
  7.2 0.0 copy-start.1
  7.2 0.0 all-reduce.10.cloned.1.call-start
  7.3 0.7 and_bitcast_fusion
  8.0 0.7 compare_and_fusion.1
  8.7 1.2 copy.19
  10.0 0.8 gather_fusion.1
  10.7 0.8 gather_fusion
  11.5 0.8 bitcast_select_fusion
  12.2 0.8 bitcast_select_fusion.1
  13.0 0.0 all-reduce.10.cloned.1.call-update
  13.0 0.0 all-reduce.6.cloned.1.call-start
  13.1 44.1 %all-reduce.10.cloned.1.call-done = (f32[256,128]{0,1:T(8,128)}, f32[256,128]{0,1:T(8,128)}) async-done(((f32[256,128]{0,1:T(8,128)}, f32[256,128]{0,1:T(8,128)}), (f32[256,128]{0,1:T(8,128)}, f32[256,128]{0,1:T(8,128)})) %all-reduce.10.cloned.1.call-update) | async-done | bytes 262160 | tf_op jit(solution)/shard_map/psum | solution.py:51
  57.2 1.9 fusion.29
  59.1 0.0 all-reduce.6.cloned.1.call-update
  59.1 0.0 all-gather.3.cloned.1.call-start
  59.2 619.8 %all-reduce.6.cloned.1.call-done = f32[128,128]{0,1:T(8,128)} async-done(((f32[128,128]{0,1:T(8,128)}), f32[128,128]{0,1:T(8,128)}) %all-reduce.6.cloned.1.call-update) | async-done | bytes 65552 | tf_op jit(solution)/shard_map/psum | solution.py:64
  679.0 0.9 copy.21
  679.9 0.9 fusion.8
  680.8 11.7 cholesky.44
  692.5 0.6 compare_reduce_fusion.1
  693.1 0.7 multiply_bitcast_fusion.2
  693.8 9.8 custom-call.6
  703.6 1.2 convolution_bitcast_fusion.2
  704.8 0.9 fusion.30
  705.7 0.0 all-gather.3.cloned.1.call-update
  705.8 0.0 all-reduce.8.cloned.1.call-start
  705.8 0.0 copy-done
  705.8 0.0 copy-done.1
  705.8 1.2 convolution_bitcast_fusion
  707.0 0.0 copy-done.3
  707.0 1.6 scatter_custom_fusion
  708.6 1.8 scatter_custom_fusion.1
  710.4 120.2 %all-gather.3.cloned.1.call-done = f32[8192,128]{1,0:T(8,128)} async-done(((f32[128,128]{1,0:T(8,128)}), f32[8192,128]{1,0:T(8,128)}) %all-gather.3.cloned.1.call-update) | async-done | bytes 4194320 | tf_op jit(solution)/shard_map/all_gather | solution.py:11
  830.7 2.4 reduce_sum.9
  833.1 0.1 copy.22
  833.2 11.7 cholesky.55
  844.9 0.7 compare_reduce_fusion
  845.7 0.6 select_bitcast_fusion
  846.3 9.8 custom-call.7
  856.1 0.3 convolution_bitcast_fusion.1
  856.4 1.3 fusion.31
  857.8 0.0 all-reduce.8.cloned.1.call-update
  857.8 0.2 copy.26
  858.0 0.7 copy.29
  858.8 0.8 copy.27
  859.5 1.5 fusion.15
  861.0 638.5 %all-reduce.8.cloned.1.call-done = (f32[1,144,512]{2,1,0:T(8,128)}, f32[128,512]{1,0:T(8,128)}) async-done(((f32[1,144,512]{2,1,0:T(8,128)}, f32[128,512]{1,0:T(8,128)}), (f32[1,144,512]{2,1,0:T(8,128)}, f32[128,512]{1,0:T(8,128)})) %all-reduce.8.cloned.1.call-update) | async-done | bytes 557072 | tf_op jit(solution)/shard_map/psum | solution.py:42
  1499.5 0.0 copy-start.2
  1499.5 1.1 copy.25
  1500.7 1.0 scatter_fusion
  1501.7 0.8 copy.28
  1502.5 2.4 fusion
  1504.9 0.0 copy-done.2
  1504.9 0.7 copy.39
  (11 shorter events, 0.2 us)
Async XLA Ops:
  7.2 698.7 %copy-start = (f32[144,256]{1,0:T(8,128)S(1)}, f32[144,256]{1,0:T(8,128)}, u32[]{:S(2)}) copy-start(f32[144,256]{1,0:T(8,128)} %param.9) | copy-start | bytes 442372
  7.2 699.8 %copy-start.3 = (s32[1,128]{1,0:T(1,128)S(1)}, s32[1,128]{1,0:T(1,128)}, u32[]{:S(2)}) copy-start(s32[1,128]{1,0:T(1,128)} %param.10) | copy-start | bytes 1540
  7.2 698.6 %copy-start.1 = (f32[256,512]{1,0:T(8,128)S(1)}, f32[256,512]{1,0:T(8,128)}, u32[]{:S(2)}) copy-start(f32[256,512]{1,0:T(8,128)} %param.8) | copy-start | bytes 1572868
  7.2 50.0 %all-reduce.10.cloned.1.call-start = ((), (), s32[]{:S(2)}) async-start(), calls=%async_computation.3 | async-start | bytes 524288 | tf_op jit(solution)/shard_map/psum | solution.py:51
  13.0 665.9 %all-reduce.6.cloned.1.call-start = ((), (), s32[]{:S(2)}) async-start(), calls=%async_computation | async-start | bytes 131072 | tf_op jit(solution)/shard_map/psum | solution.py:64
  59.1 771.5 %all-gather.3.cloned.1.call-start = ((), (), s32[]{:S(2)}) async-start(), calls=%async_computation.1 | async-start | bytes 4259840 | tf_op jit(solution)/shard_map/all_gather | solution.py:11
  705.8 793.8 %all-reduce.8.cloned.1.call-start = ((), (), s32[]{:S(2)}) async-start(), calls=%async_computation.2 | async-start | bytes 1114112 | tf_op jit(solution)/shard_map/psum | solution.py:42
  1499.5 5.4 copy-start.2
Sparse Core Ops, SparseCore 0:
  13.2 44.0 all-reduce.9
  60.6 618.3 all-reduce.5
  705.9 124.7 all-gather.2
  857.9 641.5 all-reduce.7
